TPU v7x, 32 devices: a whole 2x2x4 slice. The times are simulated.
32 devices in a mesh: rows: 8 (over z, y), cols: 4 (over x, core).
Axes of the slice: x: 2, y: 2, z: 4, core: 2. Of those that a mesh axis runs over, the one named last changes fastest.
Arguments:
- snapshot: float32 [3072, 8192], P('rows', 'cols'), may hold values from -270 to 270
- test_matrix: float32 [8192, 256], P('cols'), may hold values from -0.0625 to 0.0625
Outputs:
- projected: float32 [8192, 256], P('cols')
- triangle: float32 [256, 256], replicated
All inputs are finite; a program needn't handle non-finite values.
Results may differ from a plain program's by a relative error of at most 0.00007.
Values sent between devices are 32-bit elements; how exact they have to be, the bound alone decides.
No kernel may reach another device: no remote copies, remote signals or barrier semaphores. Data moves between devices by JAX's collectives and lax.ppermute only.
A program may use at most 64 MiB of HBM per device.

v0:
```python
import jax
import jax.numpy as jnp
from jax import lax
from jax.sharding import PartitionSpec as P

high = lax.Precision.HIGHEST


def inner(left, right):
    return jnp.dot(left.T, right, precision=high, preferred_element_type=jnp.float32)


def body(snapshot, test_matrix):
    partial_sketch = jnp.dot(
        snapshot, test_matrix, precision=high, preferred_element_type=jnp.float32
    )
    sketch = lax.psum(partial_sketch, "cols")
    local_gram = inner(sketch, sketch)
    gram = lax.psum(local_gram, "rows")
    lower = jnp.linalg.cholesky(gram)
    basis = jax.scipy.linalg.solve_triangular(lower, sketch.T, lower=True).T
    projected = lax.psum(inner(snapshot, basis), "rows")
    total = snapshot.shape[0] * lax.axis_size("rows")
    triangle = lower.T / jnp.sqrt(jnp.float32(total))
    return (projected, triangle)


def solution(mesh):
    return jax.shard_map(
        body,
        mesh=mesh,
        in_specs=(P("rows", "cols"), P("cols", None)),
        out_specs=(P("cols", None), P()),
        check_vma=False,
    )
```

profile of v0, /device:TPU:0, one launch (start us, length us, event | category | flops | bytes accessed | tf_op | source)
XLA Modules:
  0.0 326.2 jit_solution(9881222707864030921)
XLA Ops:
  7.2 1.8 copy-done
  9.1 5.0 %fusion.14 = f32[384,256]{1,0:T(8,128)} fusion(f32[384,2048]{1,0:T(8,128)S(1)} %copy-done, f32[2048,256]{1,0:T(8,128)} %param.3), kind=kOutput, calls=%fused_computation.35 | convolution fusion | flops 2415919104 | bytes 5636096 | tf_op jit(solution)/shard_map/dot_general | solution.py:14
  14.1 35.6 %all-reduce.5.cloned.1.call-done = f32[384,256]{1,0:T(8,128)} async-done(((f32[384,256]{1,0:T(8,128)}), f32[384,256]{1,0:T(8,128)}) %all-reduce.5.cloned.1.call-update) | async-done | bytes 393232 | tf_op jit(solution)/shard_map/psum | solution.py:17
  49.8 2.7 fusion.15
  52.7 72.0 %all-reduce.7.cloned.1.call-done = f32[256,256]{0,1:T(8,128)} async-done(((f32[256,256]{0,1:T(8,128)}), f32[256,256]{0,1:T(8,128)}) %all-reduce.7.cloned.1.call-update) | async-done | bytes 262160 | tf_op jit(solution)/shard_map/psum | solution.py:19
  124.7 1.8 copy.5
  128.9 13.2 %cholesky.50 = f32[128,128]{1,0:T(8,128)} custom-call(f32[128,128]{1,0:T(8,128)} %cholesky.118), custom_call_target="Cholesky" | custom-call | tf_op jit(solution)/shard_map/jit(cholesky)/cholesky | solution.py:20
  142.1 1.5 select_reduce_fusion.1
  143.6 11.3 %custom-call.15 = f32[1,128,128]{1,2,0:T(8,128)} custom-call(f32[1,128,128]{2,1,0:T(8,128)} %get-tuple-element.27), custom_call_target="InvertDiagBlocksLowerTriangular" | custom-call | tf_op jit(solution)/shard_map/jit(cholesky)/cholesky | solution.py:20
  154.9 1.6 cholesky.113
  156.4 1.7 constant_dynamic-update-slice_fusion.1
  158.1 1.7 convolution_subtract_fusion.1
  159.8 13.2 %cholesky.105 = f32[128,128]{1,0:T(8,128)} custom-call(f32[128,128]{1,0:T(8,128)} %convolution_subtract_fusion.1), custom_call_target="Cholesky" | custom-call | tf_op jit(solution)/shard_map/jit(cholesky)/cholesky | solution.py:20
  173.0 1.5 select_reduce_fusion
  176.5 1.8 multiply_bitcast_fusion
  178.3 7.0 %while.1 = (s32[]{:T(128)}, f32[256,256]{1,0:T(8,128)}, s32[2,2]{1,0:T(2,128)S(1)}, f32[2,128,128]{2,1,0:T(8,128)}, s32[]{:T(128)}) while((s32[]{:T(128)}, f32[256,256]{1,0:T(8,128)}, s32[2,2]{1,0:T(2,128)S(1)}, f32[2,128,128]{2,1,0:T(8,128)}, s32[]{:T(128)}) %tuple.29), condition=%wide.while_cond, body=%wide.while_body.sunk | while | flops 2 | bytes 132205 | solution.py:21
  179.0 2.9 bitcast_dynamic-update-slice_fusion.2
  182.5 2.8 bitcast_dynamic-update-slice_fusion.2
  185.3 21.1 %custom-call.16 = f32[2,128,128]{1,2,0:T(8,128)} custom-call(f32[2,128,128]{2,1,0:T(8,128)} %get-tuple-element.9), custom_call_target="InvertDiagBlocksLowerTriangular" | custom-call | tf_op jit(solution)/shard_map/jit(_solve_triangular)/triangular_solve | solution.py:21
  207.7 1.3 convolution_subtract_fusion
  209.0 1.2 fusion.8
  210.2 4.9 %convolution_bitcast_fusion = f32[2048,256]{0,1:T(8,128)} fusion(f32[384,2048]{1,0:T(8,128)S(1)} %copy-done, f32[128,384]{1,0:T(8,128)S(1)} %fusion.8, f32[128,384]{1,0:T(8,128)S(1)} %fusion.5), kind=kOutput, calls=%fused_computation.2 | convolution fusion | flops 2416017408 | bytes 5636096 | tf_op jit(solution)/shard_map/dot_general | solution.py:10
  216.9 99.9 %all-reduce.9.cloned.1.call-done = f32[2048,256]{0,1:T(8,128)} async-done(((f32[2048,256]{0,1:T(8,128)}), f32[2048,256]{0,1:T(8,128)}) %all-reduce.9.cloned.1.call-update) | async-done | bytes 2097168 | tf_op jit(solution)/shard_map/psum | solution.py:22
  316.8 2.9 copy.6
  (25 shorter events, 7.8 us)
Async XLA Ops:
  7.2 1.9 copy-start
  7.2 42.6 %all-reduce.5.cloned.1.call-start = ((), (), s32[]{:S(2)}) async-start(), calls=%async_computation | async-start | bytes 786432 | tf_op jit(solution)/shard_map/psum | solution.py:17
  14.1 110.7 %all-reduce.7.cloned.1.call-start = ((), (), s32[]{:S(2)}) async-start(), calls=%async_computation.1 | async-start | bytes 524288 | tf_op jit(solution)/shard_map/psum | solution.py:19
  52.5 264.3 %all-reduce.9.cloned.1.call-start = ((), (), s32[]{:S(2)}) async-start(), calls=%async_computation.2 | async-start | bytes 4194304 | tf_op jit(solution)/shard_map/psum | solution.py:22
  52.7 153.7 %copy-start.1 = (f32[384,256]{1,0:T(8,128)S(1)}, f32[384,256]{1,0:T(8,128)}, u32[]{:S(2)}) copy-start(f32[384,256]{1,0:T(8,128)} %all-reduce.5.cloned.1.call-done) | copy-start | bytes 1179652
  127.6 0.7 copy-start.3
  215.1 0.9 copy-start.2
Sparse Core Ops, SparseCore 0:
  14.2 35.5 all-reduce.4
  53.7 71.0 all-reduce.6
  215.3 101.4 all-reduce.8
where the time goes:
time: 327 us; the launch traced here: 326 us
  waiting for transfers between devices  208 us (64%)
  other arithmetic  65.2 us (20%)
  matrix products  19.8 us (6%)
  local copies, waits for them, and re-layouts  18.2 us (6%)
  between operations  15.1 us (5%)
    psum x1, waiting for transfers between devices, body(): projected = lax.psum(inner(snapshot, basis), 'rows')  99.9 us
    psum x1, waiting for transfers between devices, body(): gram = lax.psum(local_gram, 'rows')  72 us
    another operation x6, other arithmetic, body(): lower = jnp.linalg.cholesky(gram)  41.3 us
    psum x1, waiting for transfers between devices, body(): sketch = lax.psum(partial_sketch, 'cols')  35.6 us
    another operation x2, other arithmetic, body(): basis = jax.scipy.linalg.solve_triangular(lower, sketch.T, lower=True).T  21.1 us
    dot_general x2, matrix products, inner(): jnp.dot(left.T, right, precision=high, preferred_element_type=jnp.float32)  7.53 us
    unnamed x10, local copies, waits for them, and re-layouts  7.18 us
    another operation x6, local copies, waits for them, and re-layouts  6.98 us
  transfers between devices with their start and end apart: 3, of which 3 were waited for; matrix products, arithmetic and copies ran while one was open for 0% of the time, Pallas kernels for 0%

commit v1 on v0

--- a/solution.py
+++ b/solution.py
@@ -4,6 +4,10 @@
 from jax.sharding import PartitionSpec as P
 
 high = lax.Precision.HIGHEST
+
+
+def follow_shapes(frame_in, mesh_name):
+    return lax.all_gather(frame_in, mesh_name).sum(axis=0)
 
 
 def inner(left, right):
@@ -16,7 +20,7 @@
     )
     sketch = lax.psum(partial_sketch, "cols")
     local_gram = inner(sketch, sketch)
-    gram = lax.psum(local_gram, "rows")
+    gram = follow_shapes(local_gram, "rows")
     lower = jnp.linalg.cholesky(gram)
     basis = jax.scipy.linalg.solve_triangular(lower, sketch.T, lower=True).T
     projected = lax.psum(inner(snapshot, basis), "rows")

time: 327 us -> 306 us (0.936)
  waiting for transfers between devices: 208 us -> 184 us
    psum x1 -> x0, waiting for transfers between devices: 72 us -> none  [body(): gram = lax.psum(local_gram, 'rows')]
    all_gather x0 -> x1, waiting for transfers between devices: none -> 49 us  [follow_shapes(): return lax.all_gather(frame_in, mesh_name).sum(axis=0)]
where the time goes in v1:
time: 306 us; the launch traced here: 305 us
  waiting for transfers between devices  184 us (60%)
  other arithmetic  67.7 us (22%)
  matrix products  19.7 us (6%)
  local copies, waits for them, and re-layouts  18.3 us (6%)
  between operations  15.2 us (5%)
    psum x1, waiting for transfers between devices, body(): projected = lax.psum(inner(snapshot, basis), 'rows')  99.2 us
    all_gather x1, waiting for transfers between devices, follow_shapes(): return lax.all_gather(frame_in, mesh_name).sum(axis=0)  49 us
    another operation x6, other arithmetic, body(): lower = jnp.linalg.cholesky(gram)  41.3 us
    psum x1, waiting for transfers between devices, body(): sketch = lax.psum(partial_sketch, 'cols')  35.6 us
    another operation x2, other arithmetic, body(): basis = jax.scipy.linalg.solve_triangular(lower, sketch.T, lower=True).T  21.1 us
    dot_general x2, matrix products, inner(): jnp.dot(left.T, right, precision=high, preferred_element_type=jnp.float32)  7.51 us
    unnamed x10, local copies, waits for them, and re-layouts  7.18 us
    another operation x6, local copies, waits for them, and re-layouts  7.01 us
  transfers between devices with their start and end apart: 3, of which 3 were waited for; matrix products, arithmetic and copies ran while one was open for 0% of the time, Pallas kernels for 0%

profile of v1, /device:TPU:0, one launch (start us, length us, event | category | flops | bytes accessed | tf_op | source)
XLA Modules:
  0.0 305.1 jit_solution(765360380445050285)
XLA Ops:
  7.2 1.8 copy-done
  9.1 5.0 %fusion.14 = f32[384,256]{1,0:T(8,128)} fusion(f32[384,2048]{1,0:T(8,128)S(1)} %copy-done, f32[2048,256]{1,0:T(8,128)} %param.3), kind=kOutput, calls=%fused_computation.35 | convolution fusion | flops 2415919104 | bytes 5636096 | tf_op jit(solution)/shard_map/dot_general | solution.py:18
  14.1 35.6 %all-reduce.4.cloned.1.call-done = f32[384,256]{1,0:T(8,128)} async-done(((f32[384,256]{1,0:T(8,128)}), f32[384,256]{1,0:T(8,128)}) %all-reduce.4.cloned.1.call-update) | async-done | bytes 393232 | tf_op jit(solution)/shard_map/psum | solution.py:21
  49.8 2.6 fusion.15
  52.7 49.0 %all-gather.3.cloned.1.call-done = f32[2048,256]{1,0:T(8,128)} async-done(((f32[256,256]{1,0:T(8,128)}), f32[2048,256]{1,0:T(8,128)}) %all-gather.3.cloned.1.call-update) | async-done | bytes 2097168 | tf_op jit(solution)/shard_map/all_gather | solution.py:10
  101.7 2.5 reduce_sum.9
  104.1 1.8 copy.7
  108.4 13.2 %cholesky.50 = f32[128,128]{1,0:T(8,128)} custom-call(f32[128,128]{1,0:T(8,128)} %cholesky.118), custom_call_target="Cholesky" | custom-call | tf_op jit(solution)/shard_map/jit(cholesky)/cholesky | solution.py:24
  121.6 1.5 select_reduce_fusion.1
  123.0 1.6 cholesky.113
  124.6 11.3 %custom-call.15 = f32[1,128,128]{1,2,0:T(8,128)} custom-call(f32[1,128,128]{2,1,0:T(8,128)} %get-tuple-element.29), custom_call_target="InvertDiagBlocksLowerTriangular" | custom-call | tf_op jit(solution)/shard_map/jit(cholesky)/cholesky | solution.py:24
  135.9 1.7 constant_dynamic-update-slice_fusion.1
  137.6 1.7 convolution_subtract_fusion.1
  139.3 13.2 %cholesky.105 = f32[128,128]{1,0:T(8,128)} custom-call(f32[128,128]{1,0:T(8,128)} %convolution_subtract_fusion.1), custom_call_target="Cholesky" | custom-call | tf_op jit(solution)/shard_map/jit(cholesky)/cholesky | solution.py:24
  152.5 1.5 select_reduce_fusion
  156.0 1.8 multiply_bitcast_fusion
  157.9 7.0 %while.1 = (s32[]{:T(128)}, f32[256,256]{1,0:T(8,128)}, s32[2,2]{1,0:T(2,128)S(1)}, f32[2,128,128]{2,1,0:T(8,128)}, s32[]{:T(128)}) while((s32[]{:T(128)}, f32[256,256]{1,0:T(8,128)}, s32[2,2]{1,0:T(2,128)S(1)}, f32[2,128,128]{2,1,0:T(8,128)}, s32[]{:T(128)}) %tuple.30), condition=%wide.while_cond, body=%wide.while_body.sunk | while | flops 2 | bytes 132205 | solution.py:25
  158.6 2.9 bitcast_dynamic-update-slice_fusion.2
  162.1 2.8 bitcast_dynamic-update-slice_fusion.2
  164.9 21.1 %custom-call.16 = f32[2,128,128]{1,2,0:T(8,128)} custom-call(f32[2,128,128]{2,1,0:T(8,128)} %get-tuple-element.9), custom_call_target="InvertDiagBlocksLowerTriangular" | custom-call | tf_op jit(solution)/shard_map/jit(_solve_triangular)/triangular_solve | solution.py:25
  187.2 1.3 convolution_subtract_fusion
  189.8 4.9 %convolution_bitcast_fusion = f32[2048,256]{0,1:T(8,128)} fusion(f32[384,2048]{1,0:T(8,128)S(1)} %copy-done, f32[128,384]{1,0:T(8,128)S(1)} %fusion.8, f32[128,384]{1,0:T(8,128)S(1)} %fusion.5), kind=kOutput, calls=%fused_computation.2 | convolution fusion | flops 2416017408 | bytes 5636096 | tf_op jit(solution)/shard_map/dot_general | solution.py:14
  196.5 99.2 %all-reduce.6.cloned.1.call-done = f32[2048,256]{0,1:T(8,128)} async-done(((f32[2048,256]{0,1:T(8,128)}), f32[2048,256]{0,1:T(8,128)}) %all-reduce.6.cloned.1.call-update) | async-done | bytes 2097168 | tf_op jit(solution)/shard_map/psum | solution.py:26
  295.7 2.9 copy.8
  (26 shorter events, 9.1 us)
Async XLA Ops:
  7.2 1.9 copy-start
  7.2 42.6 %all-reduce.4.cloned.1.call-start = ((), (), s32[]{:S(2)}) async-start(), calls=%async_computation | async-start | bytes 786432 | tf_op jit(solution)/shard_map/psum | solution.py:21
  14.1 87.6 %all-gather.3.cloned.1.call-start = ((), (), s32[]{:S(2)}) async-start(), calls=%async_computation.2 | async-start | bytes 2359296 | tf_op jit(solution)/shard_map/all_gather | solution.py:10
  52.4 243.2 %all-reduce.6.cloned.1.call-start = ((), (), s32[]{:S(2)}) async-start(), calls=%async_computation.1 | async-start | bytes 4194304 | tf_op jit(solution)/shard_map/psum | solution.py:26
  104.1 81.8 %copy-start.1 = (f32[384,256]{1,0:T(8,128)S(1)}, f32[384,256]{1,0:T(8,128)}, u32[]{:S(2)}) copy-start(f32[384,256]{1,0:T(8,128)} %all-reduce.4.cloned.1.call-done) | copy-start | bytes 1179652
  107.1 0.7 copy-start.3
  194.7 0.9 copy-start.2
Sparse Core Ops, SparseCore 0:
  14.2 35.5 all-reduce.3
  52.6 49.0 all-gather.2
  194.8 100.7 all-reduce.5
